TPU v7x, 32 devices: a whole 2x2x4 slice. The times are simulated.
32 devices in a mesh: gx: 4 (over y, x), gy: 4 (over z), gz: 2 (over core).
Axes of the slice: x: 2, y: 2, z: 4, core: 2. Of those that a mesh axis runs over, the one named last changes fastest.
Arguments:
- fields: float32 [24, 32, 128, 256], P(None, 'gx', 'gy', 'gz'), may hold values from -8.5 to 8.5
- velocity: float32 [3, 32, 128, 256], P(None, 'gx', 'gy', 'gz'), may hold values from -0.4 to 0.4
- diffusivity: float32 [24], replicated, may hold values from 0.02 to 0.15
- weight_in: bfloat16 [24, 1600], replicated, may hold values from -1.25 to 1.25
- bias_in: float32 [1600], replicated, may hold values from -3 to 3
- weight_mid: bfloat16 [1600, 800], replicated, may hold values from -0.15625 to 0.15625
- bias_mid: float32 [800], replicated, may hold values from -3 to 3
- weight_low: bfloat16 [800, 400], replicated, may hold values from -0.21875 to 0.21875
- bias_low: float32 [400], replicated, may hold values from -3 to 3
- weight_out: bfloat16 [400, 24], replicated, may hold values from -0.3125 to 0.3125
- bias_out: float32 [24], replicated, may hold values from -3 to 3
- react_list: int32 [32, 96], P(('gx', 'gy', 'gz')), may hold values from -1 to 255, as said below
- owner_table: int32 [32, 96], P(('gx', 'gy', 'gz')), may hold values from -1 to 31, as said below
Outputs:
- updated: float32 [24, 32, 128, 256], P(None, 'gx', 'gy', 'gz')
- owner_activity: float32 [32], P(('gx', 'gy', 'gz'))
Inputs may be any that keep to these rules, and one draw needn't show every extreme that they name: `react_list`: row d lists distinct blocks of brick d, valid entries first and -1 after them; a brick lists at most 96 blocks and some brick lists exactly 96; all bricks together list 32 times the number of devices. owner_table[d, i] is -1 exactly where react_list[d, i] is, else the owner's index over gx+gy+gz; every device owns exactly 32 blocks; no brick sends more than 3 blocks to one owner, and some brick sends exactly 3 to some owner.
All inputs are finite; a program needn't handle non-finite values.
Results may differ from a plain program's by a relative error of at most 0.00058.
Values may be sent and summed in bfloat16 or wider, within the bound.
A program may use at most 256 MiB of HBM per device.

v0:
```python
import math

import jax
import jax.numpy as jnp
from jax import lax
from jax.sharding import PartitionSpec as P

OWNED = 32


viscous = 0.05
third_part = 1.0 / 3.0


def padded_2(value, sides, width):
    for axis, dim in sides:
        devices, length = (lax.axis_size(axis), value.shape[dim])
        up = [(i, (i + 1) % devices) for i in range(devices)]
        down = [(j, i) for i, j in up]
        last = lax.slice_in_dim(value, length - width, length, axis=dim)
        leading = lax.slice_in_dim(value, 0, width, axis=dim)
        before = lax.ppermute(last, axis, up)
        after = lax.ppermute(leading, axis, down)
        value = jnp.concatenate([before, value, after], axis=dim)
    return value


def pad_cells(array):
    return padded_2(array, (("gx", 1), ("gy", 2), ("gz", 3)), 1)


def interior(padded, axis_dim, offset):
    window = [slice(None)] + [slice(1, -1)] * 3
    window[axis_dim] = slice(1 + offset, padded.shape[axis_dim] - 1 + offset)
    return padded[tuple(window)]


def laplace(padded):
    summed = -6.0 * interior(padded, 1, 0)
    for axis_dim in (1, 2, 3):
        summed = summed + interior(padded, axis_dim, 1) + interior(padded, axis_dim, -1)
    return summed


def transport(padded, speeds):
    centre = interior(padded, 1, 0)
    spread = -6.0 * centre
    flux_sum = jnp.zeros_like(centre)
    for axis_dim in (1, 2, 3):
        carried = speeds[axis_dim - 1][None] * padded
        flux_sum = flux_sum + 0.5 * (
            interior(carried, axis_dim, 1) - interior(carried, axis_dim, -1)
        )
        spread = spread + interior(padded, axis_dim, 1) + interior(padded, axis_dim, -1)
    return viscous * spread - flux_sum


def network(
    block_in, weight_in, bias_in, weight_mid, bias_mid, weight_low, bias_low, weight_out, bias_out
):
    hidden = jnp.einsum("bfz,fh->bhz", block_in, weight_in, preferred_element_type=jnp.float32)
    hidden = jax.nn.silu(hidden + bias_in[None, :, None]).astype(jnp.bfloat16)
    hidden = jnp.einsum("bhz,hk->bkz", hidden, weight_mid, preferred_element_type=jnp.float32)
    hidden = jax.nn.silu(hidden + bias_mid[None, :, None]).astype(jnp.bfloat16)
    hidden = jnp.einsum("bkz,kl->blz", hidden, weight_low, preferred_element_type=jnp.float32)
    hidden = jax.nn.silu(hidden + bias_low[None, :, None]).astype(jnp.bfloat16)
    result = jnp.einsum("blz,lf->bfz", hidden, weight_out, preferred_element_type=jnp.float32)
    return result + bias_out[None, :, None]


def local(
    fields,
    velocity,
    diffusivity,
    weight_in,
    bias_in,
    weight_mid,
    bias_mid,
    weight_low,
    bias_low,
    weight_out,
    bias_out,
    react_list,
    owner_table,
):
    field_count, cells_x, cells_y, cells_z = fields.shape
    padded = pad_cells(jnp.concatenate([fields, velocity], axis=0))
    speeds = padded[field_count:]
    section_one = fields + transport(padded[:field_count], speeds)
    section_two = 0.75 * fields + 0.25 * (section_one + transport(pad_cells(section_one), speeds))
    flowed = third_part * fields + 2.0 / 3.0 * (
        section_two + transport(pad_cells(section_two), speeds)
    )
    devices = lax.axis_size(("gx", "gy", "gz"))
    block_ids = react_list[0]
    owners = owner_table[0]
    listed = block_ids.shape[0]
    capacity = (listed + devices - 1) // devices
    slots_all = devices * capacity
    block_count = cells_x * cells_y
    present = block_ids >= 0
    positions = jnp.arange(listed, dtype=jnp.int32)
    earlier = (
        (owners[None, :] == owners[:, None])
        & present[None, :]
        & (positions[None, :] < positions[:, None])
    )
    earlier_count = jnp.sum(earlier.astype(jnp.int32), axis=1)
    target_slot = jnp.where(present, owners * capacity + earlier_count, -1)
    slot_hot = (target_slot[None, :] == jnp.arange(slots_all, dtype=jnp.int32)[:, None]).astype(
        jnp.float32
    )
    block_hot = (block_ids[:, None] == jnp.arange(block_count, dtype=jnp.int32)[None, :]).astype(
        jnp.float32
    )
    routing_table = jnp.dot(slot_hot, block_hot, precision=lax.Precision.HIGHEST)
    slot_mask = (jnp.sum(slot_hot, axis=1) > 0.5).astype(jnp.int32)
    brick_blocks = flowed.reshape(field_count, block_count, cells_z).astype(jnp.bfloat16)
    outgoing = jnp.einsum(
        "sb,fbz->sfz",
        routing_table.astype(jnp.bfloat16),
        brick_blocks,
        preferred_element_type=jnp.float32,
    ).astype(jnp.bfloat16)
    outgoing = outgoing.reshape(devices, capacity, field_count, cells_z)
    slot_mask = slot_mask.reshape(devices, capacity)
    arrived, arrived_mask = (
        lax.all_to_all(outgoing, ("gx", "gy", "gz"), split_axis=0, concat_axis=0, tiled=True),
        lax.all_to_all(slot_mask, ("gx", "gy", "gz"), split_axis=0, concat_axis=0, tiled=True),
    )
    arrived = arrived.reshape(slots_all, field_count, cells_z)
    occupied = arrived_mask.reshape(slots_all)
    position = jnp.cumsum(occupied) - 1
    selector = (
        (position[None, :] == jnp.arange(OWNED, dtype=jnp.int32)[:, None])
        & (occupied[None, :] == 1)
    ).astype(jnp.float32)
    compact = jnp.einsum(
        "rs,sfz->rfz", selector.astype(jnp.bfloat16), arrived, preferred_element_type=jnp.float32
    ).astype(jnp.bfloat16)
    group_size = math.gcd(OWNED, 8)

    def run_group(blockset):
        return network(
            blockset,
            weight_in,
            bias_in,
            weight_mid,
            bias_mid,
            weight_low,
            bias_low,
            weight_out,
            bias_out,
        )

    chemistry = lax.map(
        run_group, compact.reshape(OWNED // group_size, group_size, field_count, cells_z)
    )
    chemistry = chemistry.reshape(OWNED, field_count, cells_z)
    owner_activity = (jnp.sum(jnp.mean(chemistry[:, 0, :] ** 2, axis=-1)) / 8.0).reshape(1)
    returning = jnp.einsum("rs,rfz->sfz", selector, chemistry, precision=lax.Precision.HIGHEST)
    returning = returning.reshape(devices, capacity, field_count, cells_z)
    came_back = lax.all_to_all(
        returning, ("gx", "gy", "gz"), split_axis=0, concat_axis=0, tiled=True
    )
    came_back = came_back.reshape(slots_all, field_count, cells_z)
    added = jnp.einsum("sb,sfz->fbz", routing_table, came_back, precision=lax.Precision.HIGHEST)
    added = added.reshape(field_count, cells_x, cells_y, cells_z)
    reacted = flowed + added
    rates = diffusivity[:, None, None, None]
    updated = reacted + rates * laplace(pad_cells(reacted))
    return (updated, owner_activity)


def solution(mesh):
    return jax.shard_map(
        local,
        mesh=mesh,
        in_specs=(
            P(None, "gx", "gy", "gz"),
            P(None, "gx", "gy", "gz"),
            P(),
            P(),
            P(),
            P(),
            P(),
            P(),
            P(),
            P(),
            P(),
            P(("gx", "gy", "gz"), None),
            P(("gx", "gy", "gz"), None),
        ),
        out_specs=(P(None, "gx", "gy", "gz"), P(("gx", "gy", "gz"))),
        check_vma=False,
    )
```

profile of v0, /device:TPU:0, one launch (start us, length us, event | category | flops | bytes accessed | tf_op | source)
XLA Modules:
  0.0 507.4 jit_solution(14322183739362923137)
XLA Ops:
  7.1 10.6 %collective-permute-done = f32[27,1,32,128]{3,2,1,0:T(8,128)S(1)} collective-permute-done((f32[27,1,32,128]{3,2,1,0:T(8,128)S(1)}, f32[27,1,32,128]{3,2,1,0:T(8,128)S(1)}, u32[]{:S(2)}, u32[]{:S(2)}) %collective-permute-start) | collective-permute-done | bytes 442400 | tf_op jit(solution)/shard_map/ppermute | solution.py:23
  17.7 9.3 %collective-permute-done.1 = f32[27,1,32,128]{3,2,1,0:T(8,128)S(1)} collective-permute-done((f32[27,1,32,128]{3,2,1,0:T(8,128)S(1)}, f32[27,1,32,128]{3,2,1,0:T(8,128)S(1)}, u32[]{:S(2)}, u32[]{:S(2)}) %collective-permute-start.1) | collective-permute-done | bytes 442400 | tf_op jit(solution)/shard_map/ppermute | solution.py:22
  39.8 5.9 %fusion.106 = (f32[27,10,34,1]{3,2,1,0:T(8,128)}, f32[27,10,34,1]{3,2,1,0:T(8,128)}) fusion(f32[27,10,34,128]{3,2,1,0:T(8,128)S(1)} %pad_maximum_fusion.3), kind=kLoop, calls=%fused_computation.236 | loop fusion | bytes 146880 | tf_op jit(solution)/shard_map/slice | solution.py:20
  45.7 5.1 %copy.64 = f32[27,10,34,1]{2,3,1,0:T(1,128)} copy(f32[27,10,34,1]{3,2,1,0:T(8,128)} %get-tuple-element.138) | data formatting | bytes 73440 | tf_op jit(solution)/shard_map/slice | solution.py:21
  50.8 5.1 %copy.66 = f32[27,10,34,1]{2,3,1,0:T(1,128)} copy(f32[27,10,34,1]{3,2,1,0:T(8,128)} %get-tuple-element.137) | data formatting | bytes 73440 | tf_op jit(solution)/shard_map/slice | solution.py:20
  61.1 4.8 copy.67
  71.0 9.1 %pad_maximum_fusion = f32[27,10,34,130]{3,2,1,0:T(8,128)S(1)} fusion(f32[27,10,34,1]{3,2,1,0:T(8,128)S(1)} %copy-done, f32[27,10,1,128]{3,2,1,0:T(1,128)S(1)} %copy-done.23, f32[27,1,32,128]{3,2,1,0:T(8,128)S(1)} %copy-done.9, f32[27,8,32,128]{3,2,1,0:T(8,128)S(1)} %constant_dynamic-update-slice_fusion, f32[27,1,32,128]{3,2,1,0:T(8,128)S(1)} %copy-done.11, ...), kind=kLoop, calls=%fused_computation.30 | loop fusion | flops 7160400 | bytes 9547200 | tf_op jit(solution)/shard_map/concatenate | solution.py:24
  80.1 9.9 %slice_multiply_fusion.2 = (f32[24,10,34,130]{3,2,1,0:T(8,128)}, f32[24,10,34,130]{3,2,1,0:T(8,128)}, f32[24,10,34,130]{3,2,1,0:T(8,128)}) fusion(f32[27,10,34,130]{3,2,1,0:T(8,128)S(1)} %pad_maximum_fusion, f32[10,34,130]{2,1,0:T(8,128)S(1)} %get-tuple-element.128, f32[10,34,130]{2,1,0:T(8,128)S(1)} %get-tuple-element.129, ...), kind=kLoop, calls=%fused_computation.35 | loop fusion | flops 3182400 | bytes 17503200 | tf_op jit(solution)/shard_map/mul | solution.py:50
  90.1 23.1 %fusion.69 = f32[24,8,32,128]{3,2,1,0:T(8,128)} fusion(f32[24,8,32,128]{3,2,1,0:T(8,128)} %param.15, f32[24,10,34,130]{3,2,1,0:T(8,128)} %get-tuple-element.136, f32[24,10,34,130]{3,2,1,0:T(8,128)} %get-tuple-element.135, f32[24,10,34,130]{3,2,1,0:T(8,128)} %get-tuple-element.134, f32[27,10,34,1]{3,2,1,0:T(8,128)} %copy.67, ...), kind=kLoop, calls=%fused_computation.146 | loop fusion | flops 26738688 | bytes 29939424 | tf_op jit(solution)/shard_map/add | solution.py:89
  116.6 10.0 %collective-permute-done.6 = f32[24,1,32,128]{3,2,1,0:T(8,128)S(1)} collective-permute-done((f32[24,1,32,128]{3,2,1,0:T(8,128)S(1)}, f32[24,1,32,128]{3,2,1,0:T(8,128)S(1)}, u32[]{:S(2)}, u32[]{:S(2)}) %collective-permute-start.6) | collective-permute-done | bytes 393248 | tf_op jit(solution)/shard_map/ppermute | solution.py:23
  126.5 7.4 %collective-permute-done.7 = f32[24,1,32,128]{3,2,1,0:T(8,128)S(1)} collective-permute-done((f32[24,1,32,128]{3,2,1,0:T(8,128)S(1)}, f32[24,1,32,128]{3,2,1,0:T(8,128)S(1)}, u32[]{:S(2)}, u32[]{:S(2)}) %collective-permute-start.7) | collective-permute-done | bytes 393248 | tf_op jit(solution)/shard_map/ppermute | solution.py:22
  144.3 5.4 %fusion.109 = (f32[24,10,34,1]{3,2,1,0:T(8,128)}, f32[24,10,34,1]{3,2,1,0:T(8,128)}) fusion(f32[24,10,34,128]{3,2,1,0:T(8,128)S(1)} %pad_maximum_fusion.4), kind=kLoop, calls=%fused_computation.239 | loop fusion | bytes 130560 | tf_op jit(solution)/shard_map/slice | solution.py:20
  167.0 16.5 %broadcast_multiply_fusion.5 = (f32[24,10,34,130]{3,2,1,0:T(8,128)}, f32[24,10,34,130]{3,2,1,0:T(8,128)}) fusion(f32[10,34,130]{2,1,0:T(8,128)} %copy-done.19, f32[24,10,34,1]{3,2,1,0:T(8,128)} %copy.71, f32[24,10,1,128]{3,2,1,0:T(1,128)} %copy-done.26, f32[24,1,32,128]{3,2,1,0:T(8,128)S(1)} %collective-permute-done.6, f32[24,8,32,128]{3,2,1,0:T(8,128)S(1)} %copy-done.2, ...), kind=kLoop, calls=%fused_computation.45 | loop fusion | flops 8486400 | bytes 13083200 | tf_op jit(solution)/shard_map/mul | solution.py:50
  183.5 9.8 %broadcast_multiply_fusion.1 = f32[24,10,34,130]{3,2,1,0:T(8,128)} fusion(f32[10,34,130]{2,1,0:T(8,128)S(1)} %copy-done.17, f32[24,10,34,1]{3,2,1,0:T(8,128)S(1)} %copy-done.4, f32[24,10,1,128]{3,2,1,0:T(1,128)S(1)} %copy-done.27, f32[24,1,32,128]{3,2,1,0:T(8,128)S(1)} %collective-permute-done.6, f32[24,8,32,128]{3,2,1,0:T(8,128)S(1)} %copy-done.2, ...), kind=kLoop, calls=%fused_computation.41 | loop fusion | flops 7425600 | bytes 8663200 | tf_op jit(solution)/shard_map/mul | solution.py:50
  193.4 31.1 %fusion.57 = f32[24,8,32,128]{3,2,1,0:T(8,128)} fusion(f32[24,8,32,128]{3,2,1,0:T(8,128)S(1)} %copy-done.2, f32[24,10,34,130]{3,2,1,0:T(8,128)} %broadcast_multiply_fusion.1, f32[24,10,34,130]{3,2,1,0:T(8,128)} %get-tuple-element.133, f32[24,10,34,130]{3,2,1,0:T(8,128)} %get-tuple-element.132, f32[24,10,34,1]{3,2,1,0:T(8,128)} %copy.73, ...), kind=kLoop, calls=%fused_computation.113 | loop fusion | flops 29097984 | bytes 29409024 | tf_op jit(solution)/shard_map/add | solution.py:90
  228.6 9.2 %collective-permute-done.12 = f32[24,1,32,128]{3,2,1,0:T(8,128)S(1)} collective-permute-done((f32[24,1,32,128]{3,2,1,0:T(8,128)S(1)}, f32[24,1,32,128]{3,2,1,0:T(8,128)S(1)}, u32[]{:S(2)}, u32[]{:S(2)}) %collective-permute-start.12) | collective-permute-done | bytes 393248 | tf_op jit(solution)/shard_map/ppermute | solution.py:23
  237.9 8.4 %collective-permute-done.13 = f32[24,1,32,128]{3,2,1,0:T(8,128)S(1)} collective-permute-done((f32[24,1,32,128]{3,2,1,0:T(8,128)S(1)}, f32[24,1,32,128]{3,2,1,0:T(8,128)S(1)}, u32[]{:S(2)}, u32[]{:S(2)}) %collective-permute-start.13) | collective-permute-done | bytes 393248 | tf_op jit(solution)/shard_map/ppermute | solution.py:22
  259.6 5.4 %fusion.108 = (f32[24,10,34,1]{3,2,1,0:T(8,128)}, f32[24,10,34,1]{3,2,1,0:T(8,128)}) fusion(f32[24,10,34,128]{3,2,1,0:T(8,128)S(1)} %pad_maximum_fusion.5), kind=kLoop, calls=%fused_computation.238 | loop fusion | bytes 130560 | tf_op jit(solution)/shard_map/slice | solution.py:20
  283.8 16.2 %broadcast_multiply_fusion.4 = (f32[24,10,34,130]{3,2,1,0:T(8,128)}, f32[24,10,34,130]{3,2,1,0:T(8,128)}) fusion(f32[10,34,130]{2,1,0:T(8,128)} %copy-done.19, f32[24,10,34,1]{3,2,1,0:T(8,128)} %copy.77, f32[24,10,1,128]{3,2,1,0:T(1,128)} %collective-permute-done.14, f32[24,1,32,128]{3,2,1,0:T(8,128)S(1)} %collective-permute-done.12, ...), kind=kLoop, calls=%fused_computation.44 | loop fusion | flops 8486400 | bytes 13083200 | tf_op jit(solution)/shard_map/mul | solution.py:50
  300.0 10.7 %broadcast_multiply_fusion = f32[24,10,34,130]{3,2,1,0:T(8,128)} fusion(f32[10,34,130]{2,1,0:T(8,128)S(1)} %copy-done.18, f32[24,10,34,1]{3,2,1,0:T(8,128)S(1)} %copy-done.6, f32[24,10,1,128]{3,2,1,0:T(1,128)} %collective-permute-done.14, f32[24,1,32,128]{3,2,1,0:T(8,128)S(1)} %collective-permute-done.12, f32[24,8,32,128]{3,2,1,0:T(8,128)S(1)} %copy-done.3, ...), kind=kLoop, calls=%fused_computation.40 | loop fusion | flops 7425600 | bytes 8663200 | tf_op jit(solution)/shard_map/mul | solution.py:50
  310.7 22.1 %fusion.104 = (bf16[24,8,32,128]{3,2,1,0:T(8,128)(2,1)}, f32[24,8,32,128]{3,2,1,0:T(8,128)}) fusion(f32[24,8,32,128]{3,2,1,0:T(8,128)S(1)} %copy-done.3, f32[24,10,34,130]{3,2,1,0:T(8,128)} %broadcast_multiply_fusion, f32[24,10,34,130]{3,2,1,0:T(8,128)} %get-tuple-element.131, f32[24,10,34,130]{3,2,1,0:T(8,128)} %get-tuple-element.130, ...), kind=kLoop, calls=%fused_computation.235 | loop fusion | flops 29884416 | bytes 30981888 | tf_op jit(solution)/shard_map/convert_element_type | solution.py:118
  342.1 15.5 %all-to-all-done.1 = bf16[32,3,24,128]{3,2,1,0:T(8,128)(2,1)S(1)} async-done(((bf16[32,3,24,128]{3,2,1,0:T(8,128)(2,1)}), bf16[32,3,24,128]{3,2,1,0:T(8,128)(2,1)S(1)}, u32[]{:S(2)}, u32[]{:S(2)}) %all-to-all-start.1) | async-done | bytes 589856 | tf_op jit(solution)/shard_map/all_to_all | solution.py:128
  357.9 43.8 %while.10 = (s32[]{:T(128)}, f32[4,8,24,128]{3,2,1,0:T(8,128)S(1)}, bf16[4,8,24,128]{3,1,0,2:T(8,128)(2,1)S(1)}, bf16[24,1600]{1,0:T(8,128)(2,1)S(1)}, f32[1600]...) while((s32[]{:T(128)}, f32[4,8,24,128]{3,2,1,0:T(8,128)S(1)}, ...), condition=%wide.region_4.5_spmd, body=%wide.region_3.4_spmd.sunk | while | flops 3392331776 | bytes 11750973 | solution.py:156
  361.7 7.0 %fusion.135 = bf16[8,400,128]{2,1,0:T(8,128)(2,1)S(1)} fusion(f32[800]{0:T(1024)S(1)} %get-tuple-element.260, bf16[8,1600,128]{2,1,0:T(8,128)(2,1)} %fusion.134, bf16[1600,800]{0,1:T(8,128)(2,1)} %get-tuple-element.259, f32[400]{0:T(512)S(1)} %get-tuple-element.262, bf16[800,400]{0,1:T(8,128)(2,1)S(1)} %get-tuple-element.261), kind=kOutput, calls=%fused_computation.19.clone.1 | convolution fusion | flops 3284172800 | bytes 7300800 | tf_op jit(solution)/shard_map/while/body/eval_jaxpr/bkz,kl->blz/dot_general | solution.py:65
  372.6 7.0 %fusion.135 = bf16[8,400,128]{2,1,0:T(8,128)(2,1)S(1)} fusion(f32[800]{0:T(1024)S(1)} %get-tuple-element.260, bf16[8,1600,128]{2,1,0:T(8,128)(2,1)} %fusion.134, bf16[1600,800]{0,1:T(8,128)(2,1)} %get-tuple-element.259, f32[400]{0:T(512)S(1)} %get-tuple-element.262, bf16[800,400]{0,1:T(8,128)(2,1)S(1)} %get-tuple-element.261), kind=kOutput, calls=%fused_computation.19.clone.1 | convolution fusion | flops 3284172800 | bytes 7300800 | tf_op jit(solution)/shard_map/while/body/eval_jaxpr/bkz,kl->blz/dot_general | solution.py:65
  383.6 7.0 %fusion.135 = bf16[8,400,128]{2,1,0:T(8,128)(2,1)S(1)} fusion(f32[800]{0:T(1024)S(1)} %get-tuple-element.260, bf16[8,1600,128]{2,1,0:T(8,128)(2,1)} %fusion.134, bf16[1600,800]{0,1:T(8,128)(2,1)} %get-tuple-element.259, f32[400]{0:T(512)S(1)} %get-tuple-element.262, bf16[800,400]{0,1:T(8,128)(2,1)S(1)} %get-tuple-element.261), kind=kOutput, calls=%fused_computation.19.clone.1 | convolution fusion | flops 3284172800 | bytes 7300800 | tf_op jit(solution)/shard_map/while/body/eval_jaxpr/bkz,kl->blz/dot_general | solution.py:65
  394.5 7.0 %fusion.135 = bf16[8,400,128]{2,1,0:T(8,128)(2,1)S(1)} fusion(f32[800]{0:T(1024)S(1)} %get-tuple-element.260, bf16[8,1600,128]{2,1,0:T(8,128)(2,1)} %fusion.134, bf16[1600,800]{0,1:T(8,128)(2,1)} %get-tuple-element.259, f32[400]{0:T(512)S(1)} %get-tuple-element.262, bf16[800,400]{0,1:T(8,128)(2,1)S(1)} %get-tuple-element.261), kind=kOutput, calls=%fused_computation.19.clone.1 | convolution fusion | flops 3284172800 | bytes 7300800 | tf_op jit(solution)/shard_map/while/body/eval_jaxpr/bkz,kl->blz/dot_general | solution.py:65
  403.2 32.7 %all_to_all.16 = f32[32,3,24,128]{3,2,1,0:T(8,128)S(1)} all-to-all(f32[32,3,24,128]{3,2,1,0:T(8,128)S(1)} %copy.90), channel_id=1, replica_groups=mesh['gx'=4,'gy'=4,'gz'=2] {'gx','gy','gz'}, dimensions={0} | all-to-all | bytes 2359296 | tf_op jit(solution)/shard_map/all_to_all | solution.py:163
  446.6 10.0 %collective-permute-done.18 = f32[24,1,32,128]{3,2,1,0:T(8,128)S(1)} collective-permute-done((f32[24,1,32,128]{3,2,1,0:T(8,128)S(1)}, f32[24,1,32,128]{3,2,1,0:T(8,128)S(1)}, u32[]{:S(2)}, u32[]{:S(2)}) %collective-permute-start.18) | collective-permute-done | bytes 393248 | tf_op jit(solution)/shard_map/ppermute | solution.py:23
  456.6 7.8 %collective-permute-done.19 = f32[24,1,32,128]{3,2,1,0:T(8,128)S(1)} collective-permute-done((f32[24,1,32,128]{3,2,1,0:T(8,128)S(1)}, f32[24,1,32,128]{3,2,1,0:T(8,128)S(1)}, u32[]{:S(2)}, u32[]{:S(2)}) %collective-permute-start.19) | collective-permute-done | bytes 393248 | tf_op jit(solution)/shard_map/ppermute | solution.py:22
  473.5 5.4 %fusion.107 = (f32[24,10,34,1]{3,2,1,0:T(8,128)}, f32[24,10,34,1]{3,2,1,0:T(8,128)}) fusion(f32[24,10,34,128]{3,2,1,0:T(8,128)S(1)} %pad_maximum_fusion.6), kind=kLoop, calls=%fused_computation.237 | loop fusion | bytes 130560 | tf_op jit(solution)/shard_map/slice | solution.py:21
  497.5 8.4 %fusion.32 = f32[24,8,32,128]{3,2,1,0:T(8,128)} fusion(f32[24,8,32,128]{3,2,1,0:T(8,128)S(1)} %add.218, f32[24,10,34,1]{3,2,1,0:T(8,128)} %copy.96, f32[24,10,1,128]{3,2,1,0:T(1,128)} %copy-done.32, f32[24,10,1,128]{3,2,1,0:T(1,128)} %copy-done.33, f32[24,1,32,128]{3,2,1,0:T(8,128)S(1)} %collective-permute-done.18, f32[24,1,32,128]{3,2,1,0:T(8,128)} %copy-done.21, ...), kind=kLoop, calls=%fused_computation.49 | loop fusion | flops 21233664 | bytes 7389024 | tf_op jit(solution)/shard_map/add | solution.py:171
  (204 shorter events, 161.2 us)
Async XLA Ops:
  3.1 14.5 %collective-permute-start = (f32[27,1,32,128]{3,2,1,0:T(8,128)S(1)}, f32[27,1,32,128]{3,2,1,0:T(8,128)S(1)}, u32[]{:S(2)}, u32[]{:S(2)}) collective-permute-start(f32[27,1,32,128]{3,2,1,0:T(8,128)S(1)} %get-tuple-element.154), channel_id=1, source_target_pairs={{8,0},{16,8},{24,16},{0,24},{9,1},{17,9},{25,17},{1,25},{10,2},{18... | collective-permute-start | bytes 1327112 | tf_op jit(solution)/shard_map/ppermute | solution.py:23
  7.1 19.9 %collective-permute-start.1 = (f32[27,1,32,128]{3,2,1,0:T(8,128)S(1)}, f32[27,1,32,128]{3,2,1,0:T(8,128)S(1)}, u32[]{:S(2)}, u32[]{:S(2)}) collective-permute-start(f32[27,1,32,128]{3,2,1,0:T(8,128)S(1)} %get-tuple-element.153), channel_id=1, source_target_pairs={{0,8},{8,16},{16,24},{24,0},{1,9},{9,17},{17,25},{25,1},{2,10},{10... | collective-permute-start | bytes 1327112 | tf_op jit(solution)/shard_map/ppermute | solution.py:22
  27.2 7.2 %collective-permute-start.2 = (f32[27,10,1,128]{3,2,1,0:T(1,128)S(1)}, f32[27,10,1,128]{3,2,1,0:T(1,128)S(1)}, u32[]{:S(2)}, u32[]{:S(2)}) collective-permute-start(f32[27,10,1,128]{3,2,1,0:T(1,128)S(1)} %get-tuple-element.146), channel_id=1, source_target_pairs={{2,0},{4,2},{6,4},{0,6},{3,1},{5,3},{7,5},{1,7},{10,8},{12,10},{14... | collective-permute-start | bytes 414728 | tf_op jit(solution)/shard_map/ppermute | solution.py:23
  30.8 6.8 %collective-permute-start.3 = (f32[27,10,1,128]{3,2,1,0:T(1,128)S(1)}, f32[27,10,1,128]{3,2,1,0:T(1,128)S(1)}, u32[]{:S(2)}, u32[]{:S(2)}) collective-permute-start(f32[27,10,1,128]{3,2,1,0:T(1,128)S(1)} %get-tuple-element.145), channel_id=1, source_target_pairs={{0,2},{2,4},{4,6},{6,0},{1,3},{3,5},{5,7},{7,1},{8,10},{10,12},{12... | collective-permute-start | bytes 414728 | tf_op jit(solution)/shard_map/ppermute | solution.py:22
  50.8 5.6 %collective-permute-start.4 = (f32[27,10,34,1]{2,3,1,0:T(1,128)}, f32[27,10,34,1]{2,3,1,0:T(1,128)}, u32[]{:S(2)}, u32[]{:S(2)}) collective-permute-start(f32[27,10,34,1]{2,3,1,0:T(1,128)} %copy.64), channel_id=1, source_target_pairs={{1,0},{0,1},{3,2},{2,3},{5,4},{4,5},{7,6},{6,7},{9,8},{8,9},{11,10... | collective-permute-start | bytes 110168 | tf_op jit(solution)/shard_map/ppermute | solution.py:23
  55.9 5.2 %collective-permute-start.5 = (f32[27,10,34,1]{2,3,1,0:T(1,128)}, f32[27,10,34,1]{2,3,1,0:T(1,128)}, u32[]{:S(2)}, u32[]{:S(2)}) collective-permute-start(f32[27,10,34,1]{2,3,1,0:T(1,128)} %copy.66), channel_id=1, source_target_pairs={{0,1},{1,0},{2,3},{3,2},{4,5},{5,4},{6,7},{7,6},{8,9},{9,8},{10,11... | collective-permute-start | bytes 110168 | tf_op jit(solution)/shard_map/ppermute | solution.py:22
  113.1 30.2 %copy-start.2 = (f32[24,8,32,128]{3,2,1,0:T(8,128)S(1)}, f32[24,8,32,128]{3,2,1,0:T(8,128)}, u32[]{:S(2)}) copy-start(f32[24,8,32,128]{3,2,1,0:T(8,128)} %fusion.69) | copy-start | bytes 9437188
  114.5 12.0 %collective-permute-start.6 = (f32[24,1,32,128]{3,2,1,0:T(8,128)S(1)}, f32[24,1,32,128]{3,2,1,0:T(8,128)S(1)}, u32[]{:S(2)}, u32[]{:S(2)}) collective-permute-start(f32[24,1,32,128]{3,2,1,0:T(8,128)S(1)} %get-tuple-element.160), channel_id=1, source_target_pairs={{8,0},{16,8},{24,16},{0,24},{9,1},{17,9},{25,17},{1,25},{10,2},{18... | collective-permute-start | bytes 1179656 | tf_op jit(solution)/shard_map/ppermute | solution.py:23
  116.0 18.0 %collective-permute-start.7 = (f32[24,1,32,128]{3,2,1,0:T(8,128)S(1)}, f32[24,1,32,128]{3,2,1,0:T(8,128)S(1)}, u32[]{:S(2)}, u32[]{:S(2)}) collective-permute-start(f32[24,1,32,128]{3,2,1,0:T(8,128)S(1)} %get-tuple-element.159), channel_id=1, source_target_pairs={{0,8},{8,16},{16,24},{24,0},{1,9},{9,17},{17,25},{25,1},{2,10},{10... | collective-permute-start | bytes 1179656 | tf_op jit(solution)/shard_map/ppermute | solution.py:22
  135.7 6.2 %collective-permute-start.8 = (f32[24,10,1,128]{3,2,1,0:T(1,128)S(1)}, f32[24,10,1,128]{3,2,1,0:T(1,128)S(1)}, u32[]{:S(2)}, u32[]{:S(2)}) collective-permute-start(f32[24,10,1,128]{3,2,1,0:T(1,128)S(1)} %get-tuple-element.152), channel_id=1, source_target_pairs={{2,0},{4,2},{6,4},{0,6},{3,1},{5,3},{7,5},{1,7},{10,8},{12,10},{14... | collective-permute-start | bytes 368648 | tf_op jit(solution)/shard_map/ppermute | solution.py:23
  136.7 6.7 %collective-permute-start.9 = (f32[24,10,1,128]{3,2,1,0:T(1,128)S(1)}, f32[24,10,1,128]{3,2,1,0:T(1,128)S(1)}, u32[]{:S(2)}, u32[]{:S(2)}) collective-permute-start(f32[24,10,1,128]{3,2,1,0:T(1,128)S(1)} %get-tuple-element.151), channel_id=1, source_target_pairs={{0,2},{2,4},{4,6},{6,0},{1,3},{3,5},{5,7},{7,1},{8,10},{10,12},{12... | collective-permute-start | bytes 368648 | tf_op jit(solution)/shard_map/ppermute | solution.py:22
  153.9 4.7 collective-permute-start.10
  158.1 4.7 collective-permute-start.11
  193.4 35.0 %copy-start.37 = (s32[1,96]{1,0:T(1,128)S(1)}, s32[1,96]{1,0:T(1,128)}, u32[]{:S(2)}) copy-start(s32[1,96]{1,0:T(1,128)} %param.27) | copy-start | bytes 1156
  224.5 33.3 %copy-start.3 = (f32[24,8,32,128]{3,2,1,0:T(8,128)S(1)}, f32[24,8,32,128]{3,2,1,0:T(8,128)}, u32[]{:S(2)}) copy-start(f32[24,8,32,128]{3,2,1,0:T(8,128)} %fusion.57) | copy-start | bytes 9437188
  225.8 12.0 %collective-permute-start.12 = (f32[24,1,32,128]{3,2,1,0:T(8,128)S(1)}, f32[24,1,32,128]{3,2,1,0:T(8,128)S(1)}, u32[]{:S(2)}, u32[]{:S(2)}) collective-permute-start(f32[24,1,32,128]{3,2,1,0:T(8,128)S(1)} %get-tuple-element.158), channel_id=1, source_target_pairs={{8,0},{16,8},{24,16},{0,24},{9,1},{17,9},{25,17},{1,25},{10,2},{18... | collective-permute-start | bytes 1179656 | tf_op jit(solution)/shard_map/ppermute | solution.py:23
  228.3 18.0 %collective-permute-start.13 = (f32[24,1,32,128]{3,2,1,0:T(8,128)S(1)}, f32[24,1,32,128]{3,2,1,0:T(8,128)S(1)}, u32[]{:S(2)}, u32[]{:S(2)}) collective-permute-start(f32[24,1,32,128]{3,2,1,0:T(8,128)S(1)} %get-tuple-element.157), channel_id=1, source_target_pairs={{0,8},{8,16},{16,24},{24,0},{1,9},{9,17},{17,25},{25,1},{2,10},{10... | collective-permute-start | bytes 1179656 | tf_op jit(solution)/shard_map/ppermute | solution.py:22
  249.3 6.7 %collective-permute-start.14 = (f32[24,10,1,128]{3,2,1,0:T(1,128)}, f32[24,10,1,128]{3,2,1,0:T(1,128)}, u32[]{:S(2)}, u32[]{:S(2)}) collective-permute-start(f32[24,10,1,128]{3,2,1,0:T(1,128)} %get-tuple-element.150), channel_id=1, source_target_pairs={{2,0},{4,2},{6,4},{0,6},{3,1},{5,3},{7,5},{1,7},{10,8},{12,10},{14... | collective-permute-start | bytes 368648 | tf_op jit(solution)/shard_map/ppermute | solution.py:23
  250.2 7.5 %collective-permute-start.15 = (f32[24,10,1,128]{3,2,1,0:T(1,128)}, f32[24,10,1,128]{3,2,1,0:T(1,128)}, u32[]{:S(2)}, u32[]{:S(2)}) collective-permute-start(f32[24,10,1,128]{3,2,1,0:T(1,128)} %get-tuple-element.149), channel_id=1, source_target_pairs={{0,2},{2,4},{4,6},{6,0},{1,3},{3,5},{5,7},{7,1},{8,10},{10,12},{12... | collective-permute-start | bytes 368648 | tf_op jit(solution)/shard_map/ppermute | solution.py:22
  252.1 83.8 %all-to-all-start = ((s32[32,1,3]{2,1,0:T(1,128)}), s32[32,1,3]{2,1,0:T(1,128)S(1)}, u32[]{:S(2)}, u32[]{:S(2)}) async-start(s32[32,1,3]{2,1,0:T(1,128)} %bitcast.147), calls=%async_computation | async-start | bytes 32768 | tf_op jit(solution)/shard_map/all_to_all | solution.py:129
  269.2 6.2 %collective-permute-start.16 = (f32[24,10,34,1]{2,0,3,1:T(8,128)}, f32[24,10,34,1]{2,0,3,1:T(8,128)}, u32[]{:S(2)}, u32[]{:S(2)}) collective-permute-start(f32[24,10,34,1]{2,0,3,1:T(8,128)} %copy.76), channel_id=1, source_target_pairs={{1,0},{0,1},{3,2},{2,3},{5,4},{4,5},{7,6},{6,7},{9,8},{8,9},{11,10... | collective-permute-start | bytes 97928 | tf_op jit(solution)/shard_map/ppermute | solution.py:23
  273.4 6.2 %collective-permute-start.17 = (f32[24,10,34,1]{2,0,3,1:T(8,128)}, f32[24,10,34,1]{2,0,3,1:T(8,128)}, u32[]{:S(2)}, u32[]{:S(2)}) collective-permute-start(f32[24,10,34,1]{2,0,3,1:T(8,128)} %copy.78), channel_id=1, source_target_pairs={{0,1},{1,0},{2,3},{3,2},{4,5},{5,4},{6,7},{7,6},{8,9},{9,8},{10,11... | collective-permute-start | bytes 97928 | tf_op jit(solution)/shard_map/ppermute | solution.py:22
  332.8 25.1 %copy-start.31 = (bf16[400,24]{0,1:T(8,128)(2,1)S(1)}, bf16[400,24]{0,1:T(8,128)(2,1)}, u32[]{:S(2)}) copy-start(bf16[400,24]{0,1:T(8,128)(2,1)} %param.24) | copy-start | bytes 57604
  335.8 21.8 %all-to-all-start.1 = ((bf16[32,3,24,128]{3,2,1,0:T(8,128)(2,1)}), bf16[32,3,24,128]{3,2,1,0:T(8,128)(2,1)S(1)}, u32[]{:S(2)}, u32[]{:S(2)}) async-start(bf16[32,3,24,128]{3,2,1,0:T(8,128)(2,1)} %bitcast.26), calls=%async_computation.1 | async-start | bytes 1179648 | tf_op jit(solution)/shard_map/all_to_all | solution.py:128
  401.8 34.1 %copy-start.34 = (f32[4,8,24,128]{3,2,1,0:T(8,128)}, f32[4,8,24,128]{3,2,1,0:T(8,128)S(1)}, u32[]{:S(2)}) copy-start(f32[4,8,24,128]{3,2,1,0:T(8,128)S(1)} %get-tuple-element.59) | copy-start | bytes 1179652
  401.8 34.1 %copy-start.30 = (f32[96,256]{1,0:T(8,128)S(1)}, f32[96,256]{1,0:T(8,128)}, u32[]{:S(2)}) copy-start(f32[96,256]{1,0:T(8,128)} %fusion.85) | copy-start | bytes 294916
  444.6 12.0 %collective-permute-start.18 = (f32[24,1,32,128]{3,2,1,0:T(8,128)S(1)}, f32[24,1,32,128]{3,2,1,0:T(8,128)S(1)}, u32[]{:S(2)}, u32[]{:S(2)}) collective-permute-start(f32[24,1,32,128]{3,2,1,0:T(8,128)S(1)} %get-tuple-element.156), channel_id=1, source_target_pairs={{8,0},{16,8},{24,16},{0,24},{9,1},{17,9},{25,17},{1,25},{10,2},{18... | collective-permute-start | bytes 1179656 | tf_op jit(solution)/shard_map/ppermute | solution.py:23
  445.4 18.9 %collective-permute-start.19 = (f32[24,1,32,128]{3,2,1,0:T(8,128)S(1)}, f32[24,1,32,128]{3,2,1,0:T(8,128)S(1)}, u32[]{:S(2)}, u32[]{:S(2)}) collective-permute-start(f32[24,1,32,128]{3,2,1,0:T(8,128)S(1)} %get-tuple-element.155), channel_id=1, source_target_pairs={{0,8},{8,16},{16,24},{24,0},{1,9},{9,17},{17,25},{25,1},{2,10},{10... | collective-permute-start | bytes 1179656 | tf_op jit(solution)/shard_map/ppermute | solution.py:22
  464.6 5.1 %collective-permute-start.20 = (f32[24,10,1,128]{3,2,1,0:T(1,128)S(1)}, f32[24,10,1,128]{3,2,1,0:T(1,128)S(1)}, u32[]{:S(2)}, u32[]{:S(2)}) collective-permute-start(f32[24,10,1,128]{3,2,1,0:T(1,128)S(1)} %get-tuple-element.148), channel_id=1, source_target_pairs={{2,0},{4,2},{6,4},{0,6},{3,1},{5,3},{7,5},{1,7},{10,8},{12,10},{14... | collective-permute-start | bytes 368648 | tf_op jit(solution)/shard_map/ppermute | solution.py:23
  465.9 6.7 %collective-permute-start.21 = (f32[24,10,1,128]{3,2,1,0:T(1,128)S(1)}, f32[24,10,1,128]{3,2,1,0:T(1,128)S(1)}, u32[]{:S(2)}, u32[]{:S(2)}) collective-permute-start(f32[24,10,1,128]{3,2,1,0:T(1,128)S(1)} %get-tuple-element.147), channel_id=1, source_target_pairs={{0,2},{2,4},{4,6},{6,0},{1,3},{3,5},{5,7},{7,1},{8,10},{10,12},{12... | collective-permute-start | bytes 368648 | tf_op jit(solution)/shard_map/ppermute | solution.py:22
  483.0 6.0 %collective-permute-start.22 = (f32[24,10,34,1]{2,0,3,1:T(8,128)}, f32[24,10,34,1]{2,0,3,1:T(8,128)}, u32[]{:S(2)}, u32[]{:S(2)}) collective-permute-start(f32[24,10,34,1]{2,0,3,1:T(8,128)} %copy.93), channel_id=1, source_target_pairs={{1,0},{0,1},{3,2},{2,3},{5,4},{4,5},{7,6},{6,7},{9,8},{8,9},{11,10... | collective-permute-start | bytes 97928 | tf_op jit(solution)/shard_map/ppermute | solution.py:23
  487.2 6.0 %collective-permute-start.23 = (f32[24,10,34,1]{2,0,3,1:T(8,128)}, f32[24,10,34,1]{2,0,3,1:T(8,128)}, u32[]{:S(2)}, u32[]{:S(2)}) collective-permute-start(f32[24,10,34,1]{2,0,3,1:T(8,128)} %copy.95), channel_id=1, source_target_pairs={{0,1},{1,0},{2,3},{3,2},{4,5},{5,4},{6,7},{7,6},{8,9},{9,8},{10,11... | collective-permute-start | bytes 97928 | tf_op jit(solution)/shard_map/ppermute | solution.py:22
  (40 other events, 458.9 us)
where the time goes:
time: 516 us; the launch traced here: 507 us
  other arithmetic  176 us (34%)
  local copies, waits for them, and re-layouts  107 us (21%)
  waiting for transfers between devices  107 us (21%)
  matrix products  50.6 us (10%)
  blocking collectives  32.7 us (6%)
  starting transfers between devices  30.7 us (6%)
    mul x7, other arithmetic, transport(): carried = speeds[axis_dim - 1][None] * padded  65 us
    ppermute x12, waiting for transfers between devices, padded_2(): after = lax.ppermute(leading, axis, down)  49.2 us
    ppermute x12, waiting for transfers between devices, padded_2(): before = lax.ppermute(last, axis, up)  42.2 us
    slice x11, local copies, waits for them, and re-layouts, padded_2(): last = lax.slice_in_dim(value, length - width, length, axis=dim)  37.1 us
    all_to_all x1, blocking collectives, local(): lax.all_to_all(returning, ('gx', 'gy', 'gz'), split_axis=0, concat_axis=0...  32.7 us
    add x1, other arithmetic, local(): 0.75 * fields  31.1 us
    dot_general x4, matrix products, network(): jnp.einsum('bkz,kl->blz', hidden, weight_low, preferred_element_type=jnp....  28 us
    add x1, other arithmetic, local(): section_one = fields + transport(padded[:field_count], speeds)  23.1 us
  transfers between devices with their start and end apart: 26, of which 16 were waited for; matrix products, arithmetic and copies ran while one was open for 21% of the time, Pallas kernels for 0%

commit v1 on v0

v1 whole, which is shorter than its diff:
```python
import functools

import jax
import jax.numpy as jnp
from jax import lax
from jax.experimental import pallas as pl
from jax.experimental.pallas import tpu as pltpu
from jax.sharding import PartitionSpec as P

AXES = ("gx", "gy", "gz")
MESH = pl.DeviceIdType.MESH
SUB = 8
LANES = 128
VMEM_LIMIT = 60 * 1024 * 1024


def neighbours():
    ids = {a: lax.axis_index(a) for a in AXES}
    out = []
    for a in AXES:
        n = lax.axis_size(a)
        up = dict(ids)
        up[a] = lax.rem(ids[a] + 1, n)
        down = dict(ids)
        down[a] = lax.rem(ids[a] + n - 1, n)
        out.append((tuple(up[b] for b in AXES), tuple(down[b] for b in AXES)))
    return out


def enter(near):
    barrier = pltpu.get_barrier_semaphore()
    for up, down in near:
        pl.semaphore_signal(barrier, inc=1, device_id=up, device_id_type=MESH)
        pl.semaphore_signal(barrier, inc=1, device_id=down, device_id_type=MESH)
    pl.semaphore_wait(barrier, 6)


class Halo:
    def __init__(self, near, cx, cy, xs, xr, yr, zs, zr, send_sem, recv_sem):
        self.near, self.cx, self.cy = near, cx, cy
        self.xs, self.xr, self.yr, self.zs, self.zr = xs, xr, yr, zs, zr
        self.send_sem, self.recv_sem = send_sem, recv_sem

    def copies(self, slot, u):
        cx, cy = self.cx, self.cy
        (xu, xd), (yu, yd), (zu, zd) = self.near
        plan = [
            (self.xs.at[slot, 1], self.xr.at[slot, 0], xu),
            (self.xs.at[slot, 0], self.xr.at[slot, 1], xd),
            (u.at[pl.ds(1, cx), cy], self.yr.at[slot, 0], yu),
            (u.at[pl.ds(1, cx), 1], self.yr.at[slot, 1], yd),
            (self.zs.at[slot, 1], self.zr.at[slot, 0], zu),
            (self.zs.at[slot, 0], self.zr.at[slot, 1], zd),
        ]
        return [
            pltpu.make_async_remote_copy(
                src_ref=s, dst_ref=d, send_sem=self.send_sem.at[slot, i],
                recv_sem=self.recv_sem.at[slot, i], device_id=to, device_id_type=MESH)
            for i, (s, d, to) in enumerate(plan)
        ]

    def send(self, slot, u):
        for side, x in ((0, 1), (1, self.cx)):
            for k in range(self.cy // 2):
                pair = jnp.concatenate([u[x, 1 + 2 * k], u[x, 2 + 2 * k]], axis=0)
                self.xs[slot, side, k] = pair.astype(jnp.bfloat16)
        for c in self.copies(slot, u):
            c.start()

    def receive(self, slot, u):
        for c in self.copies(slot, u):
            c.wait_recv()
        for side, x in ((0, 0), (1, self.cx + 1)):
            for k in range(self.cy // 2):
                pair = self.xr[slot, side, k].astype(jnp.float32)
                u[x, 1 + 2 * k] = pair[:SUB]
                u[x, 2 + 2 * k] = pair[SUB:]
        for side, y in ((0, 0), (1, self.cy + 1)):
            for x in range(self.cx):
                u[1 + x, y] = self.yr[slot, side, x]

    def finish(self, slot, u):
        for c in self.copies(slot, u):
            c.wait_send()


def lane_ids():
    return lax.broadcasted_iota(jnp.int32, (SUB, LANES), 1)


def face_add(lane, y, t, low, high):
    low = jnp.where(lane == y, pltpu.roll(t, y, 1) if y else t, low)
    high = jnp.where(lane == y, pltpu.roll(t, y + 1, 1), high)
    return low, high


def z_near(lane, y, t, zr_low, zr_high):
    last = pltpu.roll(zr_high, LANES - 1 - y, 1)
    first = pltpu.roll(zr_low, LANES - y, 1) if y else zr_low
    after = jnp.where(lane == LANES - 1, last, pltpu.roll(t, LANES - 1, 1))
    before = jnp.where(lane == 0, first, pltpu.roll(t, 1, 1))
    return after, before


def load_chunk(halo, slot, src, u):
    lane = lane_ids()

    def body(x, _):
        low = jnp.zeros((SUB, LANES), jnp.float32)
        high = low
        for y in range(halo.cy):
            t = src[x, y]
            u[1 + x, 1 + y] = t
            low, high = face_add(lane, y, t, low, high)
        halo.zs[slot, 0, x] = low
        halo.zs[slot, 1, x] = high
        return 0

    lax.fori_loop(0, halo.cx, body, 0)


def flow_kernel(chunks, cx, cy, q_ref, v_ref, out_ref, u_ref, w_ref, coef,
                xs, xr, yr, zs, zr, send_sem, recv_sem):
    near = neighbours()
    enter(near)
    halo = Halo(near, cx, cy, xs, xr, yr, zs, zr, send_sem, recv_sem)
    lane = lane_ids()
    v_slot = 3 * chunks
    load_chunk(halo, v_slot, v_ref, w_ref)
    halo.send(v_slot, w_ref)
    for c in range(chunks):
        load_chunk(halo, c, q_ref.at[c], u_ref.at[0, c])
        halo.send(c, u_ref.at[0, c])
    halo.receive(v_slot, w_ref)

    def make_coef(x, _):
        zl, zh = zr[v_slot, 0, x], zr[v_slot, 1, x]
        for y in range(cy):
            t = w_ref[1 + x, 1 + y]
            za, zb = z_near(lane, y, t, zl, zh)
            rows = (
                0.05 - 0.5 * w_ref[2 + x, 1 + y][0:1],
                0.05 + 0.5 * w_ref[x, 1 + y][0:1],
                0.05 - 0.5 * w_ref[1 + x, 2 + y][1:2],
                0.05 + 0.5 * w_ref[1 + x, y][1:2],
                0.05 - 0.5 * za[2:3],
                0.05 + 0.5 * zb[2:3],
            )
            for i, r in enumerate(rows):
                coef[i, x, y] = jnp.broadcast_to(r, (SUB, LANES))
        return 0

    lax.fori_loop(0, cx, make_coef, 0)

    for stage in range(3):
        weight = (1.0 / 3.0, 0.5, 1.0)[stage]
        for c in range(chunks):
            slot = stage * chunks + c
            u = u_ref.at[stage, c]
            halo.receive(slot, u)

            def body(x, _):
                zl, zh = zr[slot, 0, x], zr[slot, 1, x]
                low = jnp.zeros((SUB, LANES), jnp.float32)
                high = low
                for y in range(cy):
                    t = u[1 + x, 1 + y]
                    za, zb = z_near(lane, y, t, zl, zh)
                    s = coef[0, x, y] * u[2 + x, 1 + y] + coef[1, x, y] * u[x, 1 + y]
                    s = s + (coef[2, x, y] * u[1 + x, 2 + y] + coef[3, x, y] * u[1 + x, y])
                    s = s + (coef[4, x, y] * za + coef[5, x, y] * zb)
                    r = q_ref[c, x, y] + weight * (s - 0.3 * t)
                    if stage == 2:
                        out_ref[c, x, y] = r
                    else:
                        u_ref[stage + 1, c, 1 + x, 1 + y] = r
                        low, high = face_add(lane, y, r, low, high)
                if stage < 2:
                    zs[slot + chunks, 0, x] = low
                    zs[slot + chunks, 1, x] = high
                return 0

            lax.fori_loop(0, cx, body, 0)
            if stage < 2:
                halo.send(slot + chunks, u_ref.at[stage + 1, c])
    for stage in range(3):
        for c in range(chunks):
            halo.finish(stage * chunks + c, u_ref.at[stage, c])
    halo.finish(v_slot, w_ref)


def diffuse_kernel(chunks, cx, cy, q_ref, d_ref, out_ref, u_ref,
                   xs, xr, yr, zs, zr, send_sem, recv_sem):
    near = neighbours()
    enter(near)
    halo = Halo(near, cx, cy, xs, xr, yr, zs, zr, send_sem, recv_sem)
    lane = lane_ids()
    for c in range(chunks):
        load_chunk(halo, c, q_ref.at[c], u_ref.at[c])
        halo.send(c, u_ref.at[c])
    for c in range(chunks):
        u = u_ref.at[c]
        halo.receive(c, u)
        rate = d_ref[c]

        def body(x, _):
            zl, zh = zr[c, 0, x], zr[c, 1, x]
            for y in range(cy):
                t = u[1 + x, 1 + y]
                za, zb = z_near(lane, y, t, zl, zh)
                s = (u[2 + x, 1 + y] + u[x, 1 + y]) + (u[1 + x, 2 + y] + u[1 + x, y])
                s = s + (za + zb)
                out_ref[c, x, y] = t + rate * (s - 6.0 * t)
            return 0

        lax.fori_loop(0, cx, body, 0)
    for c in range(chunks):
        halo.finish(c, u_ref.at[c])


def chem_kernel(chunks, cy, group, list_ref, owner_ref, q_ref, w1, w2, w3, w4,
                out_ref, act_ref, x_in, h1, h2, h3, inc):
    listed = list_ref.shape[0]
    n_lanes = group * LANES
    out_ref[...] = q_ref[...]
    act_ref[...] = jnp.zeros_like(act_ref)
    flat = (lax.broadcasted_iota(jnp.int32, (SUB, LANES), 0) * LANES + lane_ids())
    row = lax.broadcasted_iota(jnp.int32, (16, n_lanes), 0)
    ones = jnp.where(row < 3, 1.0, 0.0)
    fields = chunks * SUB
    x_in[fields:fields + SUB] = ones[:SUB]
    for h in (h1, h2, h3):
        h[h.shape[0] - 16:] = ones.astype(jnp.bfloat16)
    count = lax.fori_loop(
        0, listed, lambda i, n: n + jnp.where(list_ref[i] >= 0, 1, 0), 0)

    def layer(w, src, dst, step):
        rows = w.shape[0]
        for m in range(0, rows, step):
            k = min(step, rows - m)
            h = jnp.dot(w[m:m + k], src, preferred_element_type=jnp.float32)
            dst[m:m + k] = (h + h * jnp.tanh(h)).astype(jnp.bfloat16)

    def run(g, _):
        base = g * group
        for i in range(group):
            b = jnp.maximum(list_ref[base + i], 0)
            x, y = b // cy, lax.rem(b, cy)
            for c in range(chunks):
                x_in[c * SUB:(c + 1) * SUB, i * LANES:(i + 1) * LANES] = q_ref[c, x, y]
        layer(w1, x_in[...].astype(jnp.bfloat16), h1, 400)
        layer(w2, h1[...], h2, 400)
        layer(w3, h2[...], h3, 400)
        inc[...] = jnp.dot(w4[...], h3[...], preferred_element_type=jnp.float32)
        for i in range(group):
            entry = list_ref[base + i]
            b = jnp.maximum(entry, 0)
            valid = jnp.where(entry >= 0, 1.0, 0.0)
            x, y = b // cy, lax.rem(b, cy)
            for c in range(chunks):
                t = inc[c * SUB:(c + 1) * SUB, i * LANES:(i + 1) * LANES]
                out_ref[c, x, y] = out_ref[c, x, y] + valid * t
            r = inc[0:1, i * LANES:(i + 1) * LANES]
            heat = jnp.sum(r * r, axis=1, keepdims=True) * (valid / (8.0 * LANES))
            act_ref[...] = act_ref[...] + jnp.where(flat == owner_ref[base + i], heat, 0.0)
        return 0

    lax.fori_loop(0, (count + group - 1) // group, run, 0)


def bias_columns(bias, scale):
    rest = bias * scale
    columns = []
    for _ in range(3):
        part = lax.reduce_precision(rest, 8, 7)
        rest = rest - part
        columns.append(part)
    columns = jnp.stack(columns, axis=1).astype(jnp.bfloat16)
    return columns


def folded(weight, bias, scale, pad):
    cols = bias_columns(bias, scale)
    cols = jnp.pad(cols, ((0, 0), (0, pad - 3)))
    return jnp.concatenate([weight.T * jnp.bfloat16(scale), cols], axis=1)


def vmem(n):
    return [pl.BlockSpec(memory_space=pltpu.VMEM)] * n


def halo_scratch(slots, cx, cy):
    return [
        pltpu.VMEM((slots, 2, cy // 2, 2 * SUB, LANES), jnp.bfloat16),
        pltpu.VMEM((slots, 2, cy // 2, 2 * SUB, LANES), jnp.bfloat16),
        pltpu.VMEM((slots, 2, cx, SUB, LANES), jnp.float32),
        pltpu.VMEM((slots, 2, cx, SUB, LANES), jnp.float32),
        pltpu.VMEM((slots, 2, cx, SUB, LANES), jnp.float32),
        pltpu.SemaphoreType.DMA((slots, 6)),
        pltpu.SemaphoreType.DMA((slots, 6)),
    ]


def local(fields, velocity, diffusivity, weight_in, bias_in, weight_mid, bias_mid,
          weight_low, bias_low, weight_out, bias_out, react_list, owner_table):
    nf, cx, cy, cz = fields.shape
    chunks = nf // SUB
    shape = (chunks, cx, cy, SUB, cz)
    q = fields.reshape(chunks, SUB, cx, cy, cz).transpose(0, 2, 3, 1, 4)
    v = jnp.pad(velocity, ((0, SUB - 3), (0, 0), (0, 0), (0, 0))).transpose(1, 2, 0, 3)
    padded = (cx + 2, cy + 2, SUB, cz)
    slots = 3 * chunks + 1
    flowed = pl.pallas_call(
        functools.partial(flow_kernel, chunks, cx, cy),
        out_shape=jax.ShapeDtypeStruct(shape, jnp.float32),
        in_specs=vmem(2),
        out_specs=vmem(1)[0],
        scratch_shapes=[
            pltpu.VMEM((3, chunks) + padded, jnp.float32),
            pltpu.VMEM(padded, jnp.float32),
            pltpu.VMEM((6, cx, cy, SUB, cz), jnp.float32),
        ] + halo_scratch(slots, cx, cy),
        compiler_params=pltpu.CompilerParams(
            collective_id=0, has_side_effects=True, vmem_limit_bytes=VMEM_LIMIT),
        name="flow",
    )(q, v)

    listed = react_list.shape[1]
    group = 4
    h = (weight_in.shape[1], weight_mid.shape[1], weight_low.shape[1])
    w1 = folded(weight_in, bias_in, 0.5, SUB)
    w2 = folded(weight_mid, bias_mid, 0.5, 16)
    w3 = folded(weight_low, bias_low, 0.5, 16)
    w4 = folded(weight_out, bias_out, 1.0, 16)
    smem = pl.BlockSpec(memory_space=pltpu.SMEM)
    n_lanes = group * LANES
    reacted, activity = pl.pallas_call(
        functools.partial(chem_kernel, chunks, cy, group),
        out_shape=(jax.ShapeDtypeStruct(shape, jnp.float32),
                   jax.ShapeDtypeStruct((SUB, LANES), jnp.float32)),
        in_specs=[smem, smem] + vmem(5),
        out_specs=tuple(vmem(2)),
        scratch_shapes=[
            pltpu.VMEM((nf + SUB, n_lanes), jnp.float32),
            pltpu.VMEM((h[0] + 16, n_lanes), jnp.bfloat16),
            pltpu.VMEM((h[1] + 16, n_lanes), jnp.bfloat16),
            pltpu.VMEM((h[2] + 16, n_lanes), jnp.bfloat16),
            pltpu.VMEM((nf, n_lanes), jnp.float32),
        ],
        compiler_params=pltpu.CompilerParams(vmem_limit_bytes=VMEM_LIMIT),
        name="chem",
    )(react_list[0], owner_table[0], flowed, w1, w2, w3, w4)

    devices = lax.axis_size(AXES)
    mine = activity.reshape(-1)[:devices]
    owner_activity = jnp.sum(
        lax.all_to_all(mine, AXES, split_axis=0, concat_axis=0, tiled=True)).reshape(1)

    rates = jnp.broadcast_to(diffusivity.reshape(chunks, SUB, 1), (chunks, SUB, cz))
    updated = pl.pallas_call(
        functools.partial(diffuse_kernel, chunks, cx, cy),
        out_shape=jax.ShapeDtypeStruct(shape, jnp.float32),
        in_specs=vmem(2),
        out_specs=vmem(1)[0],
        scratch_shapes=[pltpu.VMEM((chunks,) + padded, jnp.float32)]
        + halo_scratch(chunks, cx, cy),
        compiler_params=pltpu.CompilerParams(
            collective_id=1, has_side_effects=True, vmem_limit_bytes=VMEM_LIMIT),
        name="diffuse",
    )(reacted, rates)
    updated = updated.transpose(0, 3, 1, 2, 4).reshape(nf, cx, cy, cz)
    return (updated, owner_activity)


def solution(mesh):
    return jax.shard_map(
        local,
        mesh=mesh,
        in_specs=(P(None, *AXES), P(None, *AXES)) + (P(),) * 9
        + (P(AXES, None), P(AXES, None)),
        out_specs=(P(None, *AXES), P(AXES)),
        check_vma=False,
    )
```

time: 516 us -> 182 us (0.35); the launches traced: 507 us -> 182 us
  other arithmetic: 176 us -> 7.49 us
  waiting for transfers between devices: 107 us -> 0.01 us
  Pallas kernels: 0 us -> 96.8 us
  local copies, waits for them, and re-layouts: 107 us -> 16 us
  matrix products: 50.6 us -> 0 us
  blocking collectives: 32.7 us -> 0 us
  starting transfers between devices: 30.7 us -> 61 us
    pallas_call x0 -> x3, Pallas kernels: none -> 96.8 us  [the longest x1 64.8 us: local(): pl.pallas_call(functools.partial(flow_kernel, chunks, cx, cy), out_shape=...]
    ppermute x24 -> x0, waiting for transfers between devices: 91.5 us -> none  [the longest x12 49.2 us: padded_2(): after = lax.ppermute(leading, axis, down)]
    add x4 -> x0, other arithmetic: 66.2 us -> none  [the longest x1 31.1 us: local(): 0.75 * fields]
    mul x7 -> x3, other arithmetic: 65 us -> 3.25 us  [folded(): return jnp.concatenate([weight.T * jnp.bfloat16(scale), cols], axis=1)]
    slice x16 -> x0, local copies, waits for them, and re-layouts: 60.1 us -> none  [the longest x11 37.1 us: padded_2(): last = lax.slice_in_dim(value, length - width, length, axis=dim)]
    all_to_all x2 -> x1, starting transfers between devices: 8.18 us -> 61 us  [local(): lax.all_to_all(mine, AXES, split_axis=0, concat_axis=0, tiled=True)]
    dot_general x17 -> x0, matrix products: 50.6 us -> none  [the longest x4 28 us: network(): jnp.einsum('bkz,kl->blz', hidden, weight_low, preferred_element_type=jnp....]
    ppermute x8 -> x0, local copies, waits for them, and re-layouts: 34.8 us -> none  [the longest x4 17.4 us: padded_2(): after = lax.ppermute(leading, axis, down)]
  transfers between devices with their start and end apart: 26 -> 1, of which waited for: 16 -> 0; matrix products, arithmetic and copies ran while one was open for 21% -> 3% of each run, Pallas kernels for 0% -> 12%
where the time goes in v1:
time: 182 us
  Pallas kernels  96.8 us (53%)
  starting transfers between devices  61 us (34%)
  local copies, waits for them, and re-layouts  16 us (9%)
  other arithmetic  7.49 us (4%)
    pallas_call x1, Pallas kernels, local(): pl.pallas_call(functools.partial(flow_kernel, chunks, cx, cy), out_shape=...  64.8 us
    all_to_all x1, starting transfers between devices, local(): lax.all_to_all(mine, AXES, split_axis=0, concat_axis=0, tiled=True)  61 us
    pallas_call x1, Pallas kernels, local(): pl.pallas_call(functools.partial(diffuse_kernel, chunks, cx, cy), out_sha...  21.1 us
    pallas_call x1, Pallas kernels, local(): pl.pallas_call(functools.partial(chem_kernel, chunks, cy, group), out_sha...  11 us
    reshape x1, local copies, waits for them, and re-layouts, local(): q = fields.reshape(chunks, SUB, cx, cy, cz).transpose(0, 2, 3, 1, 4)  6.32 us
    transpose x1, local copies, waits for them, and re-layouts, local(): updated = updated.transpose(0, 3, 1, 2, 4).reshape(nf, cx, cy, cz)  4.09 us
  transfers between devices with their start and end apart: 1, of which 0 were waited for; matrix products, arithmetic and copies ran while one was open for 3% of the time, Pallas kernels for 12%

profile of v1, /device:TPU:0, one launch (start us, length us, event | category | flops | bytes accessed | tf_op | source)
XLA Modules:
  0.0 182.2 jit_solution(14551109588508455917)
XLA Ops:
  0.6 0.0 copy-start.1
  0.6 0.0 copy-start.4
  0.7 0.0 copy-start.2
  0.7 6.3 %copy.45 = f32[3,8,8,32,128]{4,1,3,2,0:T(8,128)} copy(f32[3,8,8,32,128]{4,3,2,1,0:T(8,128)} %bitcast.29) | data formatting | bytes 6291456 | tf_op jit(solution)/shard_map/reshape | solution.py:309
  7.0 0.0 copy-done.1
  7.0 0.3 copy.37
  7.3 1.1 pad_bitcast_fusion.v_ref
  8.3 0.0 copy-done.4
  8.4 0.0 copy-done.2
  8.5 0.9 copy.41.w1
  9.4 0.0 copy-done.5
  9.5 0.8 copy.38
  10.4 2.0 %multiply_bitcast_fusion = bf16[800,1600]{1,0:T(8,128)(2,1)S(1)} fusion(bf16[1600,800]{0,1:T(8,128)(2,1)} %param.18), kind=kLoop, calls=%fused_computation.4 | loop fusion | flops 1280000 | bytes 5120000 | tf_op jit(solution)/shard_map/mul | solution.py:285
  12.5 0.2 copy.39
  12.7 1.2 multiply_bitcast_fusion.1
  13.9 0.0 copy-done.8
  13.9 0.1 copy.40
  14.0 64.8 %flow.1.q_ref = f32[3,8,32,8,128]{4,3,2,1,0:T(8,128)} custom-call(f32[3,8,32,8,128]{4,3,2,1,0:T(8,128)} %bitcast.27, f32[8,32,8,128]{3,2,1,0:T(8,128)} %pad_bitcast_fusion.v_ref), custom_call_target="tpu_custom_call" | custom-call | tf_op jit(solution)/shard_map/flow/pallas_call | solution.py:313
  78.8 0.0 copy-start.3
  78.8 1.8 fusion.1.w2
  80.6 1.0 fusion.3.w3
  81.6 0.7 fusion.10.w4
  82.3 11.0 %chem.1 = (f32[3,8,32,8,128]{4,3,2,1,0:T(8,128)}, f32[8,128]{1,0:T(8,128)}) custom-call(s32[96]{0:T(128)} %bitcast.32, s32[96]{0:T(128)} %bitcast.33, f32[3,8,32,8,128]{4,3,2,1,0:T(8,128)} %flow.1.q_ref, bf16[1600,32]{1,0:T(8,128)(2,1)} %copy.41.w1, bf16[800,1616]{1,0:T(8,128)(2,1)} %fusion.1.w2, bf16[400,816]{1,0:T(8,128)(2,1)} %fusion.3.w3, ...), custom_call_target="tpu_custom_call" | custom-call | tf_op jit(solution)/shard_map/chem/pallas_call | solution.py:337
  93.2 0.7 slice_bitcast_fusion
  93.9 0.7 copy.43
  94.6 61.0 %all-to-all-start = ((f32[32,1,1]{2,1,0:T(1,128)}), f32[32,1,1]{2,1,0:T(1,128)S(1)}, u32[]{:S(2)}, u32[]{:S(2)}) async-start(f32[32,1,1]{2,1,0:T(1,128)} %copy.43), calls=%async_computation | async-start | bytes 32768 | tf_op jit(solution)/shard_map/all_to_all | solution.py:357
  155.6 0.1 broadcast_in_dim.7
  155.7 0.7 broadcast_in_dim.8.d_ref
  156.3 21.1 %diffuse.1 = f32[3,8,32,8,128]{4,3,2,1,0:T(8,128)} custom-call(f32[3,8,32,8,128]{4,3,2,1,0:T(8,128)} %get-tuple-element.4.q_ref, f32[3,8,128]{2,1,0:T(8,128)} %broadcast_in_dim.8.d_ref), custom_call_target="tpu_custom_call" | custom-call | tf_op jit(solution)/shard_map/diffuse/pallas_call | solution.py:360
  177.4 4.1 %copy.42 = f32[3,8,8,32,128]{4,3,2,1,0:T(8,128)} copy(f32[3,8,8,32,128]{4,1,3,2,0:T(8,128)} %bitcast.28) | data formatting | bytes 6291456 | tf_op jit(solution)/shard_map/transpose | solution.py:371
  181.5 0.0 all-to-all-done
  181.5 0.6 reduce_sum.9
  (28 shorter events, 0.2 us)
Async XLA Ops:
  0.6 6.4 %copy-start.1 = (f32[3,8,32,128]{3,2,1,0:T(8,128)S(1)}, f32[3,8,32,128]{3,2,1,0:T(8,128)}, u32[]{:S(2)}) copy-start(f32[3,8,32,128]{3,2,1,0:T(8,128)} %param.14) | copy-start | bytes 1179652
  0.6 7.7 %copy-start.4 = (f32[1600]{0:T(1024)S(1)}, f32[1600]{0:T(1024)}, u32[]{:S(2)}) copy-start(f32[1600]{0:T(1024)} %param.17) | copy-start | bytes 19204
  0.7 7.7 %copy-start.2 = (bf16[24,1600]{1,0:T(8,128)(2,1)S(1)}, bf16[24,1600]{1,0:T(8,128)(2,1)}, u32[]{:S(2)}) copy-start(bf16[24,1600]{1,0:T(8,128)(2,1)} %param.16) | copy-start | bytes 230404
  7.0 2.4 %copy-start.5 = (f32[800]{0:T(1024)S(1)}, f32[800]{0:T(1024)}, u32[]{:S(2)}) copy-start(f32[800]{0:T(1024)} %param.19) | copy-start | bytes 9604
  10.3 2.1 %copy-start.6 = (f32[400]{0:T(512)S(1)}, f32[400]{0:T(512)}, u32[]{:S(2)}) copy-start(f32[400]{0:T(512)} %param.21) | copy-start | bytes 4804
  10.3 3.5 %copy-start.8 = (f32[24]{0:T(128)S(1)}, f32[24]{0:T(128)}, u32[]{:S(2)}) copy-start(f32[24]{0:T(128)} %param.23) | copy-start | bytes 292
  14.0 64.8 %copy-start = (bf16[800,3]{1,0:T(8,128)(2,1)S(1)}, bf16[800,3]{1,0:T(8,128)(2,1)}, u32[]{:S(2)}) copy-start(bf16[800,3]{1,0:T(8,128)(2,1)} %copy.38) | copy-start | bytes 14404
  78.8 2.8 %copy-start.3 = (bf16[400,24]{0,1:T(8,128)(2,1)S(1)}, bf16[400,24]{0,1:T(8,128)(2,1)}, u32[]{:S(2)}) copy-start(bf16[400,24]{0,1:T(8,128)(2,1)} %param.22) | copy-start | bytes 57604
  82.3 73.3 %copy-start.7 = (f32[24]{0:T(128)S(1)}, f32[24]{0:T(128)}, u32[]{:S(2)}) copy-start(f32[24]{0:T(128)} %param.15) | copy-start | bytes 292
  94.6 87.0 %all-to-all-start = ((f32[32,1,1]{2,1,0:T(1,128)}), f32[32,1,1]{2,1,0:T(1,128)S(1)}, u32[]{:S(2)}, u32[]{:S(2)}) async-start(f32[32,1,1]{2,1,0:T(1,128)} %copy.43), calls=%async_computation | async-start | bytes 32768 | tf_op jit(solution)/shard_map/all_to_all | solution.py:357

commit v2 on v1

--- a/solution.py
+++ b/solution.py
@@ -27,12 +27,22 @@
     return out
 
 
-def enter(near):
+def enter(targets):
     barrier = pltpu.get_barrier_semaphore()
-    for up, down in near:
-        pl.semaphore_signal(barrier, inc=1, device_id=up, device_id_type=MESH)
-        pl.semaphore_signal(barrier, inc=1, device_id=down, device_id_type=MESH)
-    pl.semaphore_wait(barrier, 6)
+    for to in targets:
+        pl.semaphore_signal(barrier, inc=1, device_id=to, device_id_type=MESH)
+    pl.semaphore_wait(barrier, len(targets))
+
+
+def peers(axis):
+    ids = {a: lax.axis_index(a) for a in AXES}
+    n = lax.axis_size(axis)
+    out = []
+    for k in range(1, n):
+        to = dict(ids)
+        to[axis] = lax.rem(ids[axis] + k, n)
+        out.append(tuple(to[b] for b in AXES))
+    return out
 
 
 class Halo:
@@ -122,7 +132,7 @@
 def flow_kernel(chunks, cx, cy, q_ref, v_ref, out_ref, u_ref, w_ref, coef,
                 xs, xr, yr, zs, zr, send_sem, recv_sem):
     near = neighbours()
-    enter(near)
+    enter([to for pair in near for to in pair])
     halo = Halo(near, cx, cy, xs, xr, yr, zs, zr, send_sem, recv_sem)
     lane = lane_ids()
     v_slot = 3 * chunks
@@ -189,17 +199,44 @@
     halo.finish(v_slot, w_ref)
 
 
-def diffuse_kernel(chunks, cx, cy, q_ref, d_ref, out_ref, u_ref,
-                   xs, xr, yr, zs, zr, send_sem, recv_sem):
+def diffuse_kernel(chunks, cx, cy, q_ref, d_ref, act_in, out_ref, act_out, u_ref, part, got,
+                   act_send, act_recv, xs, xr, yr, zs, zr, send_sem, recv_sem):
     near = neighbours()
-    enter(near)
+    groups = [peers(a) for a in AXES[::-1]]
+    enter([to for g in groups for to in g])
     halo = Halo(near, cx, cy, xs, xr, yr, zs, zr, send_sem, recv_sem)
     lane = lane_ids()
+
+    def hops(phase):
+        return [
+            pltpu.make_async_remote_copy(
+                src_ref=part.at[phase], dst_ref=got.at[phase, k],
+                send_sem=act_send.at[phase, k], recv_sem=act_recv.at[phase, k],
+                device_id=to, device_id_type=MESH)
+            for k, to in enumerate(groups[phase])
+        ]
+
+    def gather(phase):
+        for h in hops(phase):
+            h.wait_recv()
+        total = part[phase]
+        for k in range(len(groups[phase])):
+            total = total + got[phase, k]
+        return total
+
+    part[0] = act_in[...]
     for c in range(chunks):
         load_chunk(halo, c, q_ref.at[c], u_ref.at[c])
         halo.send(c, u_ref.at[c])
+        if c == 0:
+            for h in hops(0):
+                h.start()
     for c in range(chunks):
         u = u_ref.at[c]
+        if c < len(groups) - 1:
+            part[c + 1] = gather(c)
+            for h in hops(c + 1):
+                h.start()
         halo.receive(c, u)
         rate = d_ref[c]
 
@@ -214,6 +251,21 @@
             return 0
 
         lax.fori_loop(0, cx, body, 0)
+    done = min(chunks, len(groups) - 1)
+    for phase in range(done, len(groups) - 1):
+        part[phase + 1] = gather(phase)
+        for h in hops(phase + 1):
+            h.start()
+    total = gather(len(groups) - 1)
+    me = (lax.axis_index("gx") * lax.axis_size("gy") + lax.axis_index("gy")) * lax.axis_size(
+        "gz") + lax.axis_index("gz")
+    flat = lax.broadcasted_iota(jnp.int32, (SUB, LANES), 0) * LANES + lane
+    mine = jnp.where(flat == me, total, 0.0)
+    act_out[...] = jnp.broadcast_to(
+        jnp.sum(jnp.sum(mine, axis=1, keepdims=True), axis=0, keepdims=True), (SUB, LANES))
+    for phase in range(len(groups)):
+        for h in hops(phase):
+            h.wait_send()
     for c in range(chunks):
         halo.finish(c, u_ref.at[c])
 
@@ -351,25 +403,28 @@
         name="chem",
     )(react_list[0], owner_table[0], flowed, w1, w2, w3, w4)
 
-    devices = lax.axis_size(AXES)
-    mine = activity.reshape(-1)[:devices]
-    owner_activity = jnp.sum(
-        lax.all_to_all(mine, AXES, split_axis=0, concat_axis=0, tiled=True)).reshape(1)
-
     rates = jnp.broadcast_to(diffusivity.reshape(chunks, SUB, 1), (chunks, SUB, cz))
-    updated = pl.pallas_call(
+    most = max(lax.axis_size(a) for a in AXES) - 1
+    updated, mine = pl.pallas_call(
         functools.partial(diffuse_kernel, chunks, cx, cy),
-        out_shape=jax.ShapeDtypeStruct(shape, jnp.float32),
-        in_specs=vmem(2),
-        out_specs=vmem(1)[0],
-        scratch_shapes=[pltpu.VMEM((chunks,) + padded, jnp.float32)]
+        out_shape=(jax.ShapeDtypeStruct(shape, jnp.float32),
+                   jax.ShapeDtypeStruct((SUB, LANES), jnp.float32)),
+        in_specs=vmem(3),
+        out_specs=tuple(vmem(2)),
+        scratch_shapes=[
+            pltpu.VMEM((chunks,) + padded, jnp.float32),
+            pltpu.VMEM((len(AXES), SUB, LANES), jnp.float32),
+            pltpu.VMEM((len(AXES), most, SUB, LANES), jnp.float32),
+            pltpu.SemaphoreType.DMA((len(AXES), most)),
+            pltpu.SemaphoreType.DMA((len(AXES), most)),
+        ]
         + halo_scratch(chunks, cx, cy),
         compiler_params=pltpu.CompilerParams(
             collective_id=1, has_side_effects=True, vmem_limit_bytes=VMEM_LIMIT),
         name="diffuse",
-    )(reacted, rates)
+    )(reacted, rates, activity)
     updated = updated.transpose(0, 3, 1, 2, 4).reshape(nf, cx, cy, cz)
-    return (updated, owner_activity)
+    return (updated, mine[0, 0:1])
 
 
 def solution(mesh):

time: 182 us -> 172 us (0.945)
  starting transfers between devices: 61 us -> 0 us
  Pallas kernels: 96.8 us -> 152 us
  other arithmetic: 7.49 us -> 3.95 us
    all_to_all x1 -> x0, starting transfers between devices: 61 us -> none  [local(): lax.all_to_all(mine, AXES, split_axis=0, concat_axis=0, tiled=True)]
    pallas_call x1, Pallas kernels: 11 us -> 70 us  [local(): pl.pallas_call(functools.partial(chem_kernel, chunks, cy, group), out_sha...]
    pallas_call x1, Pallas kernels: 21.1 us -> 17 us  [local(): pl.pallas_call(functools.partial(diffuse_kernel, chunks, cx, cy), out_sha...]
    mul x3, other arithmetic: 3.25 us -> 0.36 us  [folded(): return jnp.concatenate([weight.T * jnp.bfloat16(scale), cols], axis=1)]
  transfers between devices with their start and end apart: 1 -> 0, of which waited for: 0 -> 0; matrix products, arithmetic and copies ran while one was open for 3% -> 0% of each run, Pallas kernels for 12% -> 0%
where the time goes in v2:
time: 172 us
  Pallas kernels  152 us (88%)
  local copies, waits for them, and re-layouts  15.2 us (9%)
  other arithmetic  3.95 us (2%)
    pallas_call x1, Pallas kernels, local(): pl.pallas_call(functools.partial(chem_kernel, chunks, cy, group), out_sha...  70 us
    pallas_call x1, Pallas kernels, local(): pl.pallas_call(functools.partial(flow_kernel, chunks, cx, cy), out_shape=...  64.9 us
    pallas_call x1, Pallas kernels, local(): pl.pallas_call(functools.partial(diffuse_kernel, chunks, cx, cy), out_sha...  17 us
    reshape x1, local copies, waits for them, and re-layouts, local(): q = fields.reshape(chunks, SUB, cx, cy, cz).transpose(0, 2, 3, 1, 4)  6.32 us
    transpose x1, local copies, waits for them, and re-layouts, local(): updated = updated.transpose(0, 3, 1, 2, 4).reshape(nf, cx, cy, cz)  4.09 us
    concatenate x4, other arithmetic, folded(): return jnp.concatenate([weight.T * jnp.bfloat16(scale), cols], axis=1)  3.48 us

profile of v2, /device:TPU:0, one launch (start us, length us, event | category | flops | bytes accessed | tf_op | source)
XLA Modules:
  0.0 172.0 jit_solution(14913159393306051633)
XLA Ops:
  0.6 0.0 copy-start.2
  0.6 6.3 %copy.44 = f32[3,8,8,32,128]{4,1,3,2,0:T(8,128)} copy(f32[3,8,8,32,128]{4,3,2,1,0:T(8,128)} %bitcast.25) | data formatting | bytes 6291456 | tf_op jit(solution)/shard_map/reshape | solution.py:361
  7.0 0.0 copy-done.2
  7.0 0.3 copy.37
  7.2 1.1 pad_bitcast_fusion.v_ref
  8.3 64.9 %flow.1.q_ref = f32[3,8,32,8,128]{4,3,2,1,0:T(8,128)} custom-call(f32[3,8,32,8,128]{4,3,2,1,0:T(8,128)} %bitcast.24, f32[8,32,8,128]{3,2,1,0:T(8,128)} %pad_bitcast_fusion.v_ref), custom_call_target="tpu_custom_call" | custom-call | tf_op jit(solution)/shard_map/flow/pallas_call | solution.py:365
  73.2 0.0 copy-done.5
  73.3 0.0 copy-done.3
  73.4 1.0 copy.41.w1
  74.4 0.0 copy-done.6
  74.4 0.2 copy.38
  74.6 0.0 copy-done
  74.6 0.3 multiply_bitcast_fusion
  74.9 0.0 copy-start.7
  74.9 0.0 copy-start.1
  74.9 1.8 %fusion.1.w2 = bf16[800,1616]{1,0:T(8,128)(2,1)} fusion(bf16[800,3]{1,0:T(8,128)(2,1)S(1)} %copy.38, bf16[800,1600]{1,0:T(8,128)(2,1)S(1)} %multiply_bitcast_fusion), kind=kLoop, calls=%fused_computation.3 | loop fusion | flops 7756800 | bytes 5150400 | tf_op jit(solution)/shard_map/concatenate | solution.py:337
  76.8 0.0 copy-done.7
  76.8 0.2 copy.39
  77.0 0.0 copy-done.1
  77.0 0.1 multiply_bitcast_fusion.1
  77.1 1.0 fusion.3.w3
  78.1 0.0 copy-done.9
  78.1 0.1 copy.40
  78.2 0.0 copy-done.4
  78.2 0.7 fusion.10.w4
  78.9 70.0 %chem.1 = (f32[3,8,32,8,128]{4,3,2,1,0:T(8,128)}, f32[8,128]{1,0:T(8,128)}) custom-call(s32[96]{0:T(128)} %bitcast.29, s32[96]{0:T(128)} %bitcast.30, f32[3,8,32,8,128]{4,3,2,1,0:T(8,128)} %flow.1.q_ref, bf16[1600,32]{1,0:T(8,128)(2,1)} %copy.41.w1, bf16[800,1616]{1,0:T(8,128)(2,1)} %fusion.1.w2, bf16[400,816]{1,0:T(8,128)(2,1)} %fusion.3.w3, ...), custom_call_target="tpu_custom_call" | custom-call | tf_op jit(solution)/shard_map/chem/pallas_call | solution.py:389
  148.9 0.0 copy-done.8
  148.9 0.1 broadcast_in_dim.7
  149.0 0.7 broadcast_in_dim.8.d_ref
  149.7 17.0 %diffuse.1 = (f32[3,8,32,8,128]{4,3,2,1,0:T(8,128)}, f32[8,128]{1,0:T(8,128)}) custom-call(f32[3,8,32,8,128]{4,3,2,1,0:T(8,128)} %get-tuple-element.6.q_ref, f32[3,8,128]{2,1,0:T(8,128)} %broadcast_in_dim.8.d_ref, f32[8,128]{1,0:T(8,128)} %get-tuple-element.7.act_in), custom_call_target="tpu_custom_call" | custom-call | tf_op jit(solution)/shard_map/diffuse/pallas_call | solution.py:408
  166.7 4.1 %copy.42 = f32[3,8,8,32,128]{4,3,2,1,0:T(8,128)} copy(f32[3,8,8,32,128]{4,1,3,2,0:T(8,128)} %bitcast.27) | data formatting | bytes 6291456 | tf_op jit(solution)/shard_map/transpose | solution.py:426
  170.8 1.2 slice.3
  (26 shorter events, 0.2 us)
Async XLA Ops:
  0.6 6.3 %copy-start.2 = (f32[3,8,32,128]{3,2,1,0:T(8,128)S(1)}, f32[3,8,32,128]{3,2,1,0:T(8,128)}, u32[]{:S(2)}) copy-start(f32[3,8,32,128]{3,2,1,0:T(8,128)} %param.14) | copy-start | bytes 1179652
  8.3 64.9 %copy-start.5 = (f32[1600]{0:T(1024)S(1)}, f32[1600]{0:T(1024)}, u32[]{:S(2)}) copy-start(f32[1600]{0:T(1024)} %param.17) | copy-start | bytes 19204
  8.3 65.0 %copy-start.3 = (bf16[24,1600]{1,0:T(8,128)(2,1)S(1)}, bf16[24,1600]{1,0:T(8,128)(2,1)}, u32[]{:S(2)}) copy-start(bf16[24,1600]{1,0:T(8,128)(2,1)} %param.16) | copy-start | bytes 230404
  8.3 66.0 %copy-start.6 = (f32[800]{0:T(1024)S(1)}, f32[800]{0:T(1024)}, u32[]{:S(2)}) copy-start(f32[800]{0:T(1024)} %param.19) | copy-start | bytes 9604
  8.3 66.3 %copy-start = (bf16[1600,800]{0,1:T(8,128)(2,1)S(1)}, bf16[1600,800]{0,1:T(8,128)(2,1)}, u32[]{:S(2)}) copy-start(bf16[1600,800]{0,1:T(8,128)(2,1)} %param.18) | copy-start | bytes 7680004
  74.9 1.8 %copy-start.7 = (f32[400]{0:T(512)S(1)}, f32[400]{0:T(512)}, u32[]{:S(2)}) copy-start(f32[400]{0:T(512)} %param.21) | copy-start | bytes 4804
  74.9 2.1 %copy-start.1 = (bf16[800,400]{0,1:T(8,128)(2,1)S(1)}, bf16[800,400]{0,1:T(8,128)(2,1)}, u32[]{:S(2)}) copy-start(bf16[800,400]{0,1:T(8,128)(2,1)} %param.20) | copy-start | bytes 1920004
  76.8 1.3 copy-start.9
  76.8 1.4 copy-start.4
  78.9 70.1 %copy-start.8 = (f32[24]{0:T(128)S(1)}, f32[24]{0:T(128)}, u32[]{:S(2)}) copy-start(f32[24]{0:T(128)} %param.15) | copy-start | bytes 292
